TPU v7x, 32 devices: a whole 2x2x4 slice. The times are simulated.
32 devices in a mesh: groups: 2 (over x), ctx: 16 (over z, y, core).
Axes of the slice: x: 2, y: 2, z: 4, core: 2. Of those that a mesh axis runs over, the one named last changes fastest.
Arguments:
- inputs: bfloat16 [4096, 8192], P(None, ('groups', 'ctx')), parts along dimension 1, may hold values from -4 to 4
- projections: bfloat16 [512, 8192], P(None, ('groups', 'ctx')), parts along dimension 1, may hold values from -7 to 7
- step_sizes: bfloat16 [64, 8192], P(None, ('groups', 'ctx')), parts along dimension 1, may hold values from 0.0019989014 to 0.019897461
- log_rates: float32 [64], replicated, may hold values from -12 to 3
- skip_gain: float32 [64], replicated, may hold values from 0.5 to 1.5
- packing: int32 [32, 256], P(('groups', 'ctx')), parts along dimension 0, may hold values from 0 to 255, as said below
- prompt_sizes: int32 [8], P('groups'), parts along dimension 0, may hold values from 1 to 3072, 4096 in all
Outputs:
- ssd_output: bfloat16 [4096, 8192], P(None, ('groups', 'ctx')), parts along dimension 1
There are 2 independent parts, one for each index of `groups`. A program takes and returns all parts, laid end to end along the dimension named above; an argument that names none is the same for every part. Nothing has to cross between parts.
Inputs may be any that keep to these rules, and one draw needn't show every extreme that they name: `packing`: each row names every one of the loader's 256 tokens once. `prompt_sizes`: the lengths add up to 4096.
All inputs are finite; a program needn't handle non-finite values.
Results may differ from a plain program's by a relative error of at most 0.001.
The roundings to bfloat16 on the way count: a program that leaves them out, or rounds other values in their place, can miss the bound.
Values may be sent and summed in bfloat16 or wider, within the bound.
A program may use at most 320 MiB of HBM per device.

v0:
```python
import jax
import jax.numpy as jnp
from jax import lax
from jax.sharding import PartitionSpec as P

G = 4
BLOCK = 128


def carried_in(value, axis, join, neutral):
    count, mine = (lax.axis_size(axis), lax.axis_index(axis))
    pieces = jax.tree.map(lambda part: lax.all_gather(part, axis), value)
    so_far = jax.tree.map(
        lambda part, zero: jnp.full_like(part, 0) + jnp.asarray(zero, part.dtype), value, neutral
    )

    def lap(position, so_far):
        longer = join(so_far, jax.tree.map(lambda part: part[position], pieces))
        return jax.tree.map(lambda new, old: jnp.where(position < mine, new, old), longer, so_far)

    return lax.fori_loop(0, count - 1, lap, so_far)


def block_setup(block_dt, resets, decay_rate):
    step_size = block_dt.astype(jnp.float32)
    log_decay = jnp.cumsum(step_size * decay_rate[:, None], axis=1)
    before_reset = jnp.cumsum(resets) == 0
    return (step_size, log_decay, before_reset)


def block_state(block_x, block_bc, segment, setup):
    step_size, log_decay, before_reset = setup
    head_count = log_decay.shape[0]
    length = block_x.shape[1]
    per_group = head_count // G
    x_heads = block_x.reshape(G, per_group, -1, length)
    maps = block_bc.reshape(G, 2, -1, length)
    last_decay = log_decay[:, -1:]
    into_end = (
        jnp.where((segment == segment[-1])[None, :], jnp.exp(last_decay - log_decay), 0.0)
        * step_size
    )
    weighted = (x_heads * into_end.reshape(G, per_group, 1, length)).astype(jnp.bfloat16)
    block_total = jnp.einsum(
        "ghpj,gnj->ghpn", weighted, maps[:, 0], preferred_element_type=jnp.float32
    )
    block_keep = jnp.where(before_reset[-1], jnp.exp(last_decay[:, 0]), 0.0)
    return (block_keep, block_total.reshape(head_count, x_heads.shape[2], maps.shape[2]))


def block_output(block_x, block_bc, segment, setup, skip_gain, carry_in):
    step_size, log_decay, before_reset = setup
    head_count = log_decay.shape[0]
    length = block_x.shape[1]
    per_group = head_count // G
    head_width = block_x.shape[0] // head_count
    states = block_bc.shape[0] // (2 * G)
    column_index = jnp.arange(length, dtype=jnp.int32)
    allowed = (column_index[:, None] >= column_index[None, :]) & (
        segment[:, None] == segment[None, :]
    )

    def group_part(operands):
        x_group, map_group, step_group, decay_group, carry_group, skip_group = operands
        x_heads = x_group.reshape(per_group, head_width, length)
        input_map = map_group[0]
        output_map = map_group[1]
        decay_gap = decay_group[:, :, None] - decay_group[:, None, :]
        decay_mask = jnp.exp(jnp.where(allowed[None], decay_gap, -jnp.inf))
        inner_gram = jnp.einsum(
            "ni,nj->ij", output_map, input_map, preferred_element_type=jnp.float32
        )
        mixing = (inner_gram[None] * (decay_mask * step_group[:, None, :])).astype(jnp.bfloat16)
        within = jnp.einsum("hij,hpj->hpi", mixing, x_heads, preferred_element_type=jnp.float32)
        opened = jnp.where(before_reset[None, :], jnp.exp(decay_group), 0.0)
        carried = jnp.einsum(
            "hpn,ni->hpi",
            carry_group.astype(jnp.bfloat16),
            output_map,
            preferred_element_type=jnp.float32,
        )
        result = (
            within
            + carried * opened[:, None, :]
            + skip_group[:, None, None] * x_heads.astype(jnp.float32)
        )
        return result.reshape(-1, length).astype(jnp.bfloat16)

    grouped = (
        block_x.reshape(G, -1, length),
        block_bc.reshape(G, 2, states, length),
        step_size.reshape(G, per_group, length),
        log_decay.reshape(G, per_group, length),
        carry_in.reshape(G, per_group, head_width, states),
        skip_gain.reshape(G, per_group),
    )
    outputs = lax.map(group_part, grouped)
    return outputs.reshape(-1, length)


def combine(earlier, later):
    return (earlier[0] * later[0], later[0][:, None, None] * earlier[1] + later[1])


def per_device(inputs, projections, step_sizes, log_rates, skip_gain, packing, prompt_sizes):
    own_rows = inputs.shape[1]
    head_count = log_rates.shape[0]
    states = projections.shape[0] // (2 * G)
    head_width = inputs.shape[0] // head_count
    send_order = packing[0]
    owned_x, owned_bc, owned_dt = (
        lax.all_to_all(
            jnp.take(inputs, send_order, axis=1), "ctx", split_axis=1, concat_axis=1, tiled=True
        ),
        lax.all_to_all(
            jnp.take(projections, send_order, axis=1),
            "ctx",
            split_axis=1,
            concat_axis=1,
            tiled=True,
        ),
        lax.all_to_all(
            jnp.take(step_sizes, send_order, axis=1), "ctx", split_axis=1, concat_axis=1, tiled=True
        ),
    )
    position = lax.axis_index("ctx") * own_rows + jnp.arange(own_rows, dtype=jnp.int32)
    prompt_start = jnp.cumsum(prompt_sizes) - prompt_sizes
    segment = jnp.sum((position[:, None] >= prompt_start[None, :]).astype(jnp.int32), axis=1) - 1
    resets = jnp.sum((position[:, None] == prompt_start[None, :]).astype(jnp.int32), axis=1)
    decay_rate = -jnp.exp(log_rates)
    block_count = own_rows // BLOCK
    setups = []
    keeps = []
    totals = []
    dev_keep = jnp.ones((head_count,), jnp.float32)
    dev_total = jnp.zeros((head_count, head_width, states), jnp.float32)
    for block_id in range(block_count):
        lower = block_id * BLOCK
        upper = lower + BLOCK
        setup = block_setup(owned_dt[:, lower:upper], resets[lower:upper], decay_rate)
        block_keep, block_total = block_state(
            owned_x[:, lower:upper], owned_bc[:, lower:upper], segment[lower:upper], setup
        )
        setups.append(setup)
        keeps.append(block_keep)
        totals.append(block_total)
        dev_total = block_keep[:, None, None] * dev_total + block_total
        dev_keep = dev_keep * block_keep
    identity = (
        jnp.ones((head_count,), jnp.float32),
        jnp.zeros((head_count, head_width, states), jnp.float32),
    )
    carry_in = carried_in((dev_keep, dev_total), "ctx", combine, identity)[1]
    results = []
    for block_id in range(block_count):
        lower = block_id * BLOCK
        upper = lower + BLOCK
        results.append(
            block_output(
                owned_x[:, lower:upper],
                owned_bc[:, lower:upper],
                segment[lower:upper],
                setups[block_id],
                skip_gain,
                carry_in,
            )
        )
        carry_in = keeps[block_id][:, None, None] * carry_in + totals[block_id]
    return jnp.concatenate(results, axis=1)


def solution(mesh):
    in_specs = (
        P(None, ("groups", "ctx")),
        P(None, ("groups", "ctx")),
        P(None, ("groups", "ctx")),
        P(),
        P(),
        P(("groups", "ctx"), None),
        P("groups"),
    )
    out_specs = P(None, ("groups", "ctx"))
    return jax.shard_map(
        per_device, mesh=mesh, in_specs=in_specs, out_specs=out_specs, check_vma=False
    )
```

profile of v0, /device:TPU:0, one launch (start us, length us, event | category | flops | bytes accessed | tf_op | source)
XLA Modules:
  0.0 353.7 jit_solution(8487469282059257848)
XLA Ops:
  11.7 7.4 %all-to-all-start.2 = ((bf16[16,2,512]{2,1,0:T(2,128)(2,1)}), bf16[16,2,512]{2,1,0:T(2,128)(2,1)S(1)}, u32[]{:S(2)}, u32[]{:S(2)}) async-start(bf16[16,2,512]{2,1,0:T(2,128)(2,1)} %reshape.453), calls=%async_computation.2 | async-start | bytes 65536 | tf_op jit(solution)/shard_map/all_to_all | solution.py:122
  22.2 2.9 copy.56
  25.1 3.2 gather_fusion
  28.3 6.0 %all-to-all-start.1 = ((bf16[512,16,16]{0,2,1:T(8,128)(2,1)}), bf16[512,16,16]{0,2,1:T(8,128)(2,1)S(1)}, u32[]{:S(2)}, u32[]{:S(2)}) async-start(bf16[512,16,16]{0,2,1:T(8,128)(2,1)} %broadcast_select_fusion.1), calls=%async_computation.1 | async-start | bytes 524288 | tf_op jit(solution)/shard_map/all_to_all | solution.py:115
  34.3 3.2 broadcast_select_fusion
  37.5 6.8 %all-to-all-done.1 = bf16[512,16,16]{0,2,1:T(8,128)(2,1)S(1)} async-done(((bf16[512,16,16]{0,2,1:T(8,128)(2,1)}), bf16[512,16,16]{0,2,1:T(8,128)(2,1)S(1)}, u32[]{:S(2)}, u32[]{:S(2)}) %all-to-all-start.1) | async-done | bytes 262176 | tf_op jit(solution)/shard_map/all_to_all | solution.py:115
  44.3 3.7 %all-to-all-start = ((bf16[4096,16,16]{0,2,1:T(8,128)(2,1)}), bf16[4096,16,16]{0,2,1:T(8,128)(2,1)S(1)}, u32[]{:S(2)}, u32[]{:S(2)}) async-start(bf16[4096,16,16]{0,2,1:T(8,128)(2,1)} %broadcast_select_fusion), calls=%async_computation | async-start | bytes 4194304 | tf_op jit(solution)/shard_map/all_to_all | solution.py:112
  58.6 30.3 %all-to-all-done = bf16[4096,16,16]{0,2,1:T(8,128)(2,1)S(1)} async-done(((bf16[4096,16,16]{0,2,1:T(8,128)(2,1)}), bf16[4096,16,16]{0,2,1:T(8,128)(2,1)S(1)}, u32[]{:S(2)}, u32[]{:S(2)}) %all-to-all-start) | async-done | bytes 2097184 | tf_op jit(solution)/shard_map/all_to_all | solution.py:112
  98.2 41.0 %all-reduce = f32[1024]{0:T(1024)S(1)} all-reduce(f32[1024]{0:T(1024)S(1)} %dynamic-update-slice), channel_id=2, replica_groups=mesh['groups'=2,'ctx'=16] {'ctx'}, use_global_device_ids=true, to_apply=%add | all-reduce | flops 1024 | bytes 8192
  140.4 130.0 %all-gather.3.cloned.1.call-done = f32[16,64,64,64]{3,2,1,0:T(8,128)} async-done(((f32[1,64,64,64]{3,2,1,0:T(8,128)}), f32[16,64,64,64]{3,2,1,0:T(8,128)}) %all-gather.3.cloned.1.call-update) | async-done | bytes 16777232 | tf_op jit(solution)/shard_map/all_gather | solution.py:12
  270.4 41.8 %while.38 = (s32[]{:T(128)}, f32[64,64,64]{2,1,0:T(8,128)S(1)}, s32[]{:T(128)}, f32[16,64]{1,0:T(8,128)}, f32[16,64,64,64]{3,2,1,0:T(8,128)}, /*index=5*/s32[]{:T(128)}, s32[]{:T(128)}) while((s32[]{:T(128)}, f32[64,64,64]{2,1,0:T(8,128)S(1)}, s32[]{:T(128)}, f32[16,64]{1,0:T(8,128)}, f32[16,64,64,64]{3,2,1,0:T(8,128)}, ...), condition=%wide.region_8.9_spmd.clone, body=%wide.region_7.8_spmd.clone.sunk | while | flops 1048580 | bytes 3146601 | solution.py:21
  271.1 2.1 fusion.105
  273.9 2.1 fusion.105
  276.7 2.1 fusion.105
  279.5 2.1 fusion.105
  285.0 2.1 fusion.105
  287.8 2.1 fusion.105
  293.4 2.1 fusion.105
  296.2 2.1 fusion.105
  299.0 2.1 fusion.105
  314.6 17.8 %while.36 = (s32[]{:T(128)}, bf16[4,1024,128]{2,1,0:T(8,128)(2,1)}, bf16[4,1024,128]{2,1,0:T(8,128)(2,1)}, bf16[4,2,64,128]{3,2,1,0:T(8,128)(2,1)S(1)}, f32[4,16...) while((s32[]{:T(128)}, bf16[4,1024,128]{2,1,0:T(8,128)(2,1)}, ...), condition=%wide.region_10.11_spmd.clone, body=%wide.region_9.10_spmd.clone.sunk | while | flops 54577152 | bytes 3428257 | solution.py:97
  332.4 2.9 bitcast_add_fusion.1
  335.4 8.6 %while.37 = (s32[]{:T(128)}, bf16[4,1024,128]{2,1,0:T(8,128)(2,1)S(1)}, bf16[4,1024,128]{2,1,0:T(8,128)(2,1)S(1)}, bf16[4,2,64,128]{3,2,1,0:T(8,128)(2,1)S(1)}, ...) while((s32[]{:T(128)}, ...), condition=%wide.region_12.13_spmd.clone, body=%wide.region_11.12_spmd.clone.sunk | while | flops 54577152 | bytes 3427749 | solution.py:97
  344.1 2.8 pad_maximum_fusion
  (188 shorter events, 79.8 us)
Async XLA Ops:
  11.7 16.6 %all-to-all-start.2 = ((bf16[16,2,512]{2,1,0:T(2,128)(2,1)}), bf16[16,2,512]{2,1,0:T(2,128)(2,1)S(1)}, u32[]{:S(2)}, u32[]{:S(2)}) async-start(bf16[16,2,512]{2,1,0:T(2,128)(2,1)} %reshape.453), calls=%async_computation.2 | async-start | bytes 65536 | tf_op jit(solution)/shard_map/all_to_all | solution.py:122
  28.3 16.0 %all-to-all-start.1 = ((bf16[512,16,16]{0,2,1:T(8,128)(2,1)}), bf16[512,16,16]{0,2,1:T(8,128)(2,1)S(1)}, u32[]{:S(2)}, u32[]{:S(2)}) async-start(bf16[512,16,16]{0,2,1:T(8,128)(2,1)} %broadcast_select_fusion.1), calls=%async_computation.1 | async-start | bytes 524288 | tf_op jit(solution)/shard_map/all_to_all | solution.py:115
  37.5 10.6 %copy-start.12 = (s32[4]{0:T(128)S(1)}, s32[4]{0:T(128)}, u32[]{:S(2)}) copy-start(s32[4]{0:T(128)} %param.19) | copy-start | bytes 52
  37.5 13.4 %copy-start.13 = (f32[64]{0:T(128)S(1)}, f32[64]{0:T(128)}, u32[]{:S(2)}) copy-start(f32[64]{0:T(128)} %param.16) | copy-start | bytes 772
  44.3 44.6 %all-to-all-start = ((bf16[4096,16,16]{0,2,1:T(8,128)(2,1)}), bf16[4096,16,16]{0,2,1:T(8,128)(2,1)S(1)}, u32[]{:S(2)}, u32[]{:S(2)}) async-start(bf16[4096,16,16]{0,2,1:T(8,128)(2,1)} %broadcast_select_fusion), calls=%async_computation | async-start | bytes 4194304 | tf_op jit(solution)/shard_map/all_to_all | solution.py:112
  48.0 222.4 %all-gather.3.cloned.1.call-start = ((), (), s32[]{:S(2)}) async-start(), calls=%async_computation.3 | async-start | bytes 35651584 | tf_op jit(solution)/shard_map/all_gather | solution.py:12
  50.2 0.7 copy-start.4
  90.1 1.2 copy-start.2
  90.7 1.7 copy-start.1
  91.9 0.8 copy-start.3
  92.4 1.3 copy-start
  92.4 1.3 copy-start.8
  92.4 1.3 copy-start.11
  95.4 0.7 copy-start.10
  95.4 1.3 copy-start.14
  95.4 2.5 copy-start.5
  95.4 2.5 copy-start.9
  312.2 2.4 copy-start.6
  314.6 17.8 %copy-start.7 = (f32[64]{0:T(128)S(1)}, f32[64]{0:T(128)}, u32[]{:S(2)}) copy-start(f32[64]{0:T(128)} %get-tuple-element.354) | copy-start | bytes 772
Sparse Core Ops, SparseCore 0:
  95.5 174.8 all-gather.2
where the time goes:
time: 356 us; the launch traced here: 354 us
  waiting for transfers between devices  167 us (47%)
  other arithmetic  54.9 us (15%)
  local copies, waits for them, and re-layouts  42.3 us (12%)
  blocking collectives  41 us (12%)
  starting transfers between devices  17.2 us (5%)
  matrix products  16 us (4%)
  between operations  14.3 us (4%)
    all_gather x1, waiting for transfers between devices, carried_in(): pieces = jax.tree.map(lambda part: lax.all_gather(part, axis), value)  130 us
    unnamed x1, blocking collectives  41 us
    select_n x15, other arithmetic, lap(): jnp.where(position < mine, new, old)  31.1 us
    all_to_all x1, waiting for transfers between devices, per_device(): lax.all_to_all(jnp.take(inputs, send_order, axis=1), 'ctx', split_axis=1,...  30.3 us
    unnamed x43, local copies, waits for them, and re-layouts  10.6 us
    mul x15, local copies, waits for them, and re-layouts, combine(): later[0][:, None, None] * earlier[1] + later[1]  10.4 us
    dot_general x8, matrix products, group_part(): jnp.einsum('hpn,ni->hpi', carry_group.astype(jnp.bfloat16), output_map, p...  9.35 us
    all_to_all x1, starting transfers between devices, per_device(): lax.all_to_all(jnp.take(step_sizes, send_order, axis=1), 'ctx', split_axi...  7.41 us
  transfers between devices with their start and end apart: 4, of which 3 were waited for; matrix products, arithmetic and copies ran while one was open for 7% of the time, Pallas kernels for 0%

commit v1 on v0

--- a/solution.py
+++ b/solution.py
@@ -1,10 +1,35 @@
+import functools
 import jax
 import jax.numpy as jnp
 from jax import lax
 from jax.sharding import PartitionSpec as P
+from jax.lax import axis_index, axis_size, ppermute
 
 G = 4
 BLOCK = 128
+
+
+def cover_slices(local, along_axis):
+    latest, reached = (axis_size(along_axis), axis_index(along_axis))
+    d_next = list(local.shape)
+    ready = local.shape[1] // latest
+    d_next[1] = ready
+    p_next = d_next[1]
+    d_next[1] = p_next * latest
+    ii = 0
+    field_out = jnp.zeros(d_next, local.dtype)
+    while ii < latest:
+        work_now = lax.dynamic_slice_in_dim(local, (reached ^ ii) * ready, ready, axis=1)
+        if ii:
+            work_now = ppermute(work_now, along_axis, [(h, h ^ ii) for h in range(latest)])
+        field_out = lax.dynamic_update_slice_in_dim(
+            field_out, work_now, (reached ^ ii) * p_next, axis=1
+        )
+        ii = ii + 1
+    return field_out
+
+
+serve_stocks = functools.partial(cover_slices, along_axis="ctx")
 
 
 def carried_in(value, axis, join, neutral):
@@ -109,9 +134,7 @@
     head_width = inputs.shape[0] // head_count
     send_order = packing[0]
     owned_x, owned_bc, owned_dt = (
-        lax.all_to_all(
-            jnp.take(inputs, send_order, axis=1), "ctx", split_axis=1, concat_axis=1, tiled=True
-        ),
+        serve_stocks(jnp.take(inputs, send_order, axis=1)),
         lax.all_to_all(
             jnp.take(projections, send_order, axis=1),
             "ctx",

time: 356 us -> 388 us (1.090)
  local copies, waits for them, and re-layouts: 42.3 us -> 82.8 us
  starting transfers between devices: 17.2 us -> 38 us
  waiting for transfers between devices: 167 us -> 149 us
  blocking collectives: 41 us -> 33.5 us
    dynamic_update_slice x0 -> x17, local copies, waits for them, and re-layouts: none -> 39.4 us  [cover_slices(): lax.dynamic_update_slice_in_dim(field_out, work_now, (reached ^ ii) * p_n...]
    all_to_all x1 -> x0, waiting for transfers between devices: 30.3 us -> none  [per_device(): lax.all_to_all(jnp.take(inputs, send_order, axis=1), 'ctx', split_axis=1,...]
    ppermute x0 -> x15, starting transfers between devices: none -> 25.9 us  [cover_slices(): ppermute(work_now, along_axis, [(h, h ^ ii) for h in range(latest)])]
    ppermute x0 -> x15, waiting for transfers between devices: none -> 10.9 us  [cover_slices(): ppermute(work_now, along_axis, [(h, h ^ ii) for h in range(latest)])]
    all_gather x1, waiting for transfers between devices: 130 us -> 138 us  [carried_in(): pieces = jax.tree.map(lambda part: lax.all_gather(part, axis), value)]
    unnamed x1, blocking collectives: 41 us -> 33.5 us
    all_to_all x1, waiting for transfers between devices: 6.84 us -> 0.01 us  [per_device(): lax.all_to_all(jnp.take(projections, send_order, axis=1), 'ctx', split_ax...]
    unnamed x43 -> x37, local copies, waits for them, and re-layouts: 10.6 us -> 9.01 us
  transfers between devices with their start and end apart: 4 -> 18, of which waited for: 3 -> 3; matrix products, arithmetic and copies ran while one was open for 7% -> 15% of each run, Pallas kernels for 0% -> 0%
where the time goes in v1:
time: 388 us; the launch traced here: 385 us
  waiting for transfers between devices  149 us (38%)
  local copies, waits for them, and re-layouts  82.8 us (21%)
  other arithmetic  51.2 us (13%)
  starting transfers between devices  38 us (10%)
  blocking collectives  33.5 us (9%)
  matrix products  16 us (4%)
  between operations  14.4 us (4%)
    all_gather x1, waiting for transfers between devices, carried_in(): pieces = jax.tree.map(lambda part: lax.all_gather(part, axis), value)  138 us
    dynamic_update_slice x17, local copies, waits for them, and re-layouts, cover_slices(): lax.dynamic_update_slice_in_dim(field_out, work_now, (reached ^ ii) * p_n...  39.4 us
    unnamed x1, blocking collectives  33.5 us
    select_n x15, other arithmetic, lap(): jnp.where(position < mine, new, old)  31.1 us
    ppermute x15, starting transfers between devices, cover_slices(): ppermute(work_now, along_axis, [(h, h ^ ii) for h in range(latest)])  25.9 us
    ppermute x15, waiting for transfers between devices, cover_slices(): ppermute(work_now, along_axis, [(h, h ^ ii) for h in range(latest)])  10.9 us
    mul x15, local copies, waits for them, and re-layouts, combine(): later[0][:, None, None] * earlier[1] + later[1]  10.3 us
    dot_general x8, matrix products, group_part(): jnp.einsum('hpn,ni->hpi', carry_group.astype(jnp.bfloat16), output_map, p...  9.35 us
  transfers between devices with their start and end apart: 18, of which 3 were waited for; matrix products, arithmetic and copies ran while one was open for 15% of the time, Pallas kernels for 0%

profile of v1, /device:TPU:0, one launch (start us, length us, event | category | flops | bytes accessed | tf_op | source)
XLA Modules:
  0.0 385.3 jit_solution(63622977947277200)
XLA Ops:
  7.2 2.9 copy.60
  10.3 3.2 gather_fusion
  17.0 2.5 collective-permute-start.1
  24.5 6.1 %all-to-all-start.1 = ((bf16[16,2,512]{2,1,0:T(2,128)(2,1)}), bf16[16,2,512]{2,1,0:T(2,128)(2,1)S(1)}, u32[]{:S(2)}, u32[]{:S(2)}) async-start(bf16[16,2,512]{2,1,0:T(2,128)(2,1)} %reshape.446), calls=%async_computation.1 | async-start | bytes 65536 | tf_op jit(solution)/shard_map/all_to_all | solution.py:145
  38.3 6.0 %all-to-all-start = ((bf16[512,16,16]{0,2,1:T(8,128)(2,1)}), bf16[512,16,16]{0,2,1:T(8,128)(2,1)S(1)}, u32[]{:S(2)}, u32[]{:S(2)}) async-start(bf16[512,16,16]{0,2,1:T(8,128)(2,1)} %broadcast_select_fusion.1), calls=%async_computation | async-start | bytes 524288 | tf_op jit(solution)/shard_map/all_to_all | solution.py:138
  48.8 2.9 collective-permute-start.5
  54.8 2.4 collective-permute-start.7
  60.6 3.5 collective-permute-start.9
  66.4 3.3 collective-permute-start.11
  70.3 6.1 %collective-permute-done.7 = bf16[4096,16]{0,1:T(8,128)(2,1)S(1)} collective-permute-done((bf16[4096,16]{0,1:T(8,128)(2,1)}, bf16[4096,16]{0,1:T(8,128)(2,1)S(1)}, u32[]{:S(2)}, u32[]{:S(2)}) %collective-permute-start.7) | collective-permute-done | bytes 131104 | tf_op jit(solution)/shard_map/ppermute | solution.py:24
  76.4 2.6 collective-permute-start.12
  79.7 3.3 collective-permute-start.13
  83.7 4.8 %collective-permute-done.9 = bf16[4096,16]{0,1:T(8,128)(2,1)S(1)} collective-permute-done((bf16[4096,16]{0,1:T(8,128)(2,1)S(1)}, bf16[4096,16]{0,1:T(8,128)(2,1)S(1)}, u32[]{:S(2)}, u32[]{:S(2)}) %collective-permute-start.9) | collective-permute-done | bytes 131104 | tf_op jit(solution)/shard_map/ppermute | solution.py:24
  88.5 2.7 collective-permute-start.14
  93.8 4.1 %copy.61 = bf16[4096,256]{1,0:T(8,128)(2,1)} copy(bf16[4096,256]{0,1:T(8,128)(2,1)} %constant_dynamic-update-slice_fusion) | data formatting | bytes 4194304 | tf_op jit(solution)/shard_map/dynamic_update_slice | solution.py:25
  98.4 11.1 %dynamic_update_slice.69 = bf16[4096,256]{1,0:T(8,128)(2,1)} dynamic-update-slice(bf16[4096,256]{1,0:T(8,128)(2,1)} %copy.61, bf16[4096,16]{1,0:T(8,128)(2,1)S(1)} %copy.62, s32[]{:T(128)} %constant.135.clone.1, s32[]{:T(128)S(6)} %select_n.215) | dynamic-update-slice | bytes 262148 | tf_op jit(solution)/shard_map/dynamic_update_slice | solution.py:25
  109.9 11.1 %dynamic_update_slice.70 = bf16[4096,256]{1,0:T(8,128)(2,1)} dynamic-update-slice(bf16[4096,256]{1,0:T(8,128)(2,1)} %dynamic_update_slice.69, bf16[4096,16]{1,0:T(8,128)(2,1)S(1)} %copy.63, s32[]{:T(128)} %constant.135.clone.1, s32[]{:T(128)S(6)} %select_n.216) | dynamic-update-slice | bytes 262148 | tf_op jit(solution)/shard_map/dynamic_update_slice | solution.py:25
  129.8 33.5 %all-reduce = f32[1024]{0:T(1024)S(1)} all-reduce(f32[1024]{0:T(1024)S(1)} %dynamic-update-slice), channel_id=2, replica_groups=mesh['groups'=2,'ctx'=16] {'ctx'}, use_global_device_ids=true, to_apply=%add | all-reduce | flops 1024 | bytes 8192
  164.5 137.7 %all-gather.3.cloned.1.call-done = f32[16,64,64,64]{3,2,1,0:T(8,128)} async-done(((f32[1,64,64,64]{3,2,1,0:T(8,128)}), f32[16,64,64,64]{3,2,1,0:T(8,128)}) %all-gather.3.cloned.1.call-update) | async-done | bytes 16777232 | tf_op jit(solution)/shard_map/all_gather | solution.py:37
  302.2 41.7 %while.38 = (s32[]{:T(128)}, f32[64,64,64]{2,1,0:T(8,128)S(1)}, s32[]{:T(128)}, f32[16,64]{1,0:T(8,128)}, f32[16,64,64,64]{3,2,1,0:T(8,128)}, /*index=5*/s32[]{:T(128)}, s32[]{:T(128)}) while((s32[]{:T(128)}, f32[64,64,64]{2,1,0:T(8,128)S(1)}, s32[]{:T(128)}, f32[16,64]{1,0:T(8,128)}, f32[16,64,64,64]{3,2,1,0:T(8,128)}, ...), condition=%wide.region_8.9_spmd.clone, body=%wide.region_7.8_spmd.clone.sunk | while | flops 1048580 | bytes 3146601 | solution.py:46
  346.3 17.8 %while.36 = (s32[]{:T(128)}, bf16[4,1024,128]{2,1,0:T(8,128)(2,1)}, bf16[4,1024,128]{2,1,0:T(8,128)(2,1)}, bf16[4,2,64,128]{3,2,1,0:T(8,128)(2,1)S(1)}, f32[4,16...) while((s32[]{:T(128)}, bf16[4,1024,128]{2,1,0:T(8,128)(2,1)}, ...), condition=%wide.region_10.11_spmd.clone, body=%wide.region_9.10_spmd.clone.sunk | while | flops 54577152 | bytes 3428257 | solution.py:122
  364.1 2.9 bitcast_add_fusion.1
  367.1 8.6 %while.37 = (s32[]{:T(128)}, bf16[4,1024,128]{2,1,0:T(8,128)(2,1)S(1)}, bf16[4,1024,128]{2,1,0:T(8,128)(2,1)S(1)}, bf16[4,2,64,128]{3,2,1,0:T(8,128)(2,1)S(1)}, ...) while((s32[]{:T(128)}, ...), condition=%wide.region_12.13_spmd.clone, body=%wide.region_11.12_spmd.clone.sunk | while | flops 54577152 | bytes 3427749 | solution.py:122
  375.7 2.8 pad_maximum_fusion
  (232 shorter events, 114.9 us)
Async XLA Ops:
  15.3 6.1 %copy-start.5 = (bf16[64,256]{1,0:T(8,128)(2,1)S(1)}, bf16[64,256]{1,0:T(8,128)(2,1)}, u32[]{:S(2)}) copy-start(bf16[64,256]{1,0:T(8,128)(2,1)} %param.15) | copy-start | bytes 98308
  15.3 15.3 %copy-start.10 = (s32[4]{0:T(128)S(1)}, s32[4]{0:T(128)}, u32[]{:S(2)}) copy-start(s32[4]{0:T(128)} %param.19) | copy-start | bytes 52
  15.3 16.8 %copy-start.3 = (bf16[512,256]{1,0:T(8,128)(2,1)S(1)}, bf16[512,256]{1,0:T(8,128)(2,1)}, u32[]{:S(2)}) copy-start(bf16[512,256]{1,0:T(8,128)(2,1)} %param.14) | copy-start | bytes 786436
  16.5 32.3 %collective-permute-start = (bf16[4096,16]{0,1:T(8,128)(2,1)}, bf16[4096,16]{0,1:T(8,128)(2,1)}, u32[]{:S(2)}, u32[]{:S(2)}) collective-permute-start(bf16[4096,16]{0,1:T(8,128)(2,1)} %get-tuple-element.371), channel_id=1, source_target_pairs={{0,1},{1,0},{2,3},{3,2},{4,5},{5,4},{6,7},{7,6},{8,9},{9,8},{10,11... | collective-permute-start | bytes 393224 | tf_op jit(solution)/shard_map/ppermute | solution.py:24
  17.0 36.3 %collective-permute-start.1 = (bf16[4096,16]{0,1:T(8,128)(2,1)}, bf16[4096,16]{0,1:T(8,128)(2,1)}, u32[]{:S(2)}, u32[]{:S(2)}) collective-permute-start(bf16[4096,16]{0,1:T(8,128)(2,1)} %get-tuple-element.370), channel_id=1, source_target_pairs={{0,2},{1,3},{2,0},{3,1},{4,6},{5,7},{6,4},{7,5},{8,10},{9,11},{10,... | collective-permute-start | bytes 393224 | tf_op jit(solution)/shard_map/ppermute | solution.py:24
  19.5 35.4 %collective-permute-start.2 = (bf16[4096,16]{0,1:T(8,128)(2,1)}, bf16[4096,16]{0,1:T(8,128)(2,1)}, u32[]{:S(2)}, u32[]{:S(2)}) collective-permute-start(bf16[4096,16]{0,1:T(8,128)(2,1)} %get-tuple-element.369), channel_id=1, source_target_pairs={{0,3},{1,2},{2,1},{3,0},{4,7},{5,6},{6,5},{7,4},{8,11},{9,10},{10,... | collective-permute-start | bytes 393224 | tf_op jit(solution)/shard_map/ppermute | solution.py:24
  19.6 39.2 %collective-permute-start.3 = (bf16[4096,16]{0,1:T(8,128)(2,1)}, bf16[4096,16]{0,1:T(8,128)(2,1)}, u32[]{:S(2)}, u32[]{:S(2)}) collective-permute-start(bf16[4096,16]{0,1:T(8,128)(2,1)} %get-tuple-element.368), channel_id=1, source_target_pairs={{0,4},{1,5},{2,6},{3,7},{4,0},{5,1},{6,2},{7,3},{8,12},{9,13},{10,... | collective-permute-start | bytes 393224 | tf_op jit(solution)/shard_map/ppermute | solution.py:24
  21.4 39.2 %collective-permute-start.4 = (bf16[4096,16]{0,1:T(8,128)(2,1)}, bf16[4096,16]{0,1:T(8,128)(2,1)}, u32[]{:S(2)}, u32[]{:S(2)}) collective-permute-start(bf16[4096,16]{0,1:T(8,128)(2,1)} %get-tuple-element.367), channel_id=1, source_target_pairs={{0,5},{1,4},{2,7},{3,6},{4,1},{5,0},{6,3},{7,2},{8,13},{9,12},{10,... | collective-permute-start | bytes 393224 | tf_op jit(solution)/shard_map/ppermute | solution.py:24
  24.5 13.8 %all-to-all-start.1 = ((bf16[16,2,512]{2,1,0:T(2,128)(2,1)}), bf16[16,2,512]{2,1,0:T(2,128)(2,1)S(1)}, u32[]{:S(2)}, u32[]{:S(2)}) async-start(bf16[16,2,512]{2,1,0:T(2,128)(2,1)} %reshape.446), calls=%async_computation.1 | async-start | bytes 65536 | tf_op jit(solution)/shard_map/all_to_all | solution.py:145
  33.4 3.8 copy-start.11
  34.2 26.4 %copy-start.4 = (bf16[4096,16]{0,1:T(8,128)(2,1)S(1)}, bf16[4096,16]{0,1:T(8,128)(2,1)}, u32[]{:S(2)}) copy-start(bf16[4096,16]{0,1:T(8,128)(2,1)} %get-tuple-element.362) | copy-start | bytes 393220
  38.3 84.4 %all-to-all-start = ((bf16[512,16,16]{0,2,1:T(8,128)(2,1)}), bf16[512,16,16]{0,2,1:T(8,128)(2,1)S(1)}, u32[]{:S(2)}, u32[]{:S(2)}) async-start(bf16[512,16,16]{0,2,1:T(8,128)(2,1)} %broadcast_select_fusion.1), calls=%async_computation | async-start | bytes 524288 | tf_op jit(solution)/shard_map/all_to_all | solution.py:138
  44.3 257.9 %all-gather.3.cloned.1.call-start = ((), (), s32[]{:S(2)}) async-start(), calls=%async_computation.2 | async-start | bytes 35651584 | tf_op jit(solution)/shard_map/all_gather | solution.py:37
  48.8 16.9 %collective-permute-start.5 = (bf16[4096,16]{0,1:T(8,128)(2,1)}, bf16[4096,16]{0,1:T(8,128)(2,1)S(1)}, u32[]{:S(2)}, u32[]{:S(2)}) collective-permute-start(bf16[4096,16]{0,1:T(8,128)(2,1)} %get-tuple-element.366), channel_id=1, source_target_pairs={{0,6},{1,7},{2,4},{3,5},{4,2},{5,3},{6,0},{7,1},{8,14},{9,15},{10,... | collective-permute-start | bytes 393224 | tf_op jit(solution)/shard_map/ppermute | solution.py:24
  53.3 13.2 %collective-permute-start.6 = (bf16[4096,16]{0,1:T(8,128)(2,1)}, bf16[4096,16]{0,1:T(8,128)(2,1)S(1)}, u32[]{:S(2)}, u32[]{:S(2)}) collective-permute-start(bf16[4096,16]{0,1:T(8,128)(2,1)} %get-tuple-element.365), channel_id=1, source_target_pairs={{0,7},{1,6},{2,5},{3,4},{4,3},{5,2},{6,1},{7,0},{8,15},{9,14},{10,... | collective-permute-start | bytes 393224 | tf_op jit(solution)/shard_map/ppermute | solution.py:24
  54.8 21.6 %collective-permute-start.7 = (bf16[4096,16]{0,1:T(8,128)(2,1)}, bf16[4096,16]{0,1:T(8,128)(2,1)S(1)}, u32[]{:S(2)}, u32[]{:S(2)}) collective-permute-start(bf16[4096,16]{0,1:T(8,128)(2,1)} %get-tuple-element.364), channel_id=1, source_target_pairs={{0,8},{1,9},{2,10},{3,11},{4,12},{5,13},{6,14},{7,15},{8,0},{9,1},... | collective-permute-start | bytes 393224 | tf_op jit(solution)/shard_map/ppermute | solution.py:24
  58.8 20.9 %collective-permute-start.8 = (bf16[4096,16]{0,1:T(8,128)(2,1)}, bf16[4096,16]{0,1:T(8,128)(2,1)S(1)}, u32[]{:S(2)}, u32[]{:S(2)}) collective-permute-start(bf16[4096,16]{0,1:T(8,128)(2,1)} %get-tuple-element.363), channel_id=1, source_target_pairs={{0,9},{1,8},{2,11},{3,10},{4,13},{5,12},{6,15},{7,14},{8,1},{9,0},... | collective-permute-start | bytes 393224 | tf_op jit(solution)/shard_map/ppermute | solution.py:24
  60.6 27.9 %collective-permute-start.9 = (bf16[4096,16]{0,1:T(8,128)(2,1)S(1)}, bf16[4096,16]{0,1:T(8,128)(2,1)S(1)}, u32[]{:S(2)}, u32[]{:S(2)}) collective-permute-start(bf16[4096,16]{0,1:T(8,128)(2,1)S(1)} %copy-done.4), channel_id=1, source_target_pairs={{0,10},{1,11},{2,8},{3,9},{4,14},{5,15},{6,12},{7,13},{8,2},{9,3},... | collective-permute-start | bytes 393224 | tf_op jit(solution)/shard_map/ppermute | solution.py:24
  65.7 26.1 %collective-permute-start.10 = (bf16[4096,16]{0,1:T(8,128)(2,1)S(1)}, bf16[4096,16]{0,1:T(8,128)(2,1)S(1)}, u32[]{:S(2)}, u32[]{:S(2)}) collective-permute-start(bf16[4096,16]{0,1:T(8,128)(2,1)S(1)} %get-tuple-element.361), channel_id=1, source_target_pairs={{0,11},{1,10},{2,9},{3,8},{4,15},{5,14},{6,13},{7,12},{8,3},{9,2},... | collective-permute-start | bytes 393224 | tf_op jit(solution)/shard_map/ppermute | solution.py:24
  66.4 26.1 %collective-permute-start.11 = (bf16[4096,16]{0,1:T(8,128)(2,1)S(1)}, bf16[4096,16]{0,1:T(8,128)(2,1)S(1)}, u32[]{:S(2)}, u32[]{:S(2)}) collective-permute-start(bf16[4096,16]{0,1:T(8,128)(2,1)S(1)} %get-tuple-element.360), channel_id=1, source_target_pairs={{0,12},{1,13},{2,14},{3,15},{4,8},{5,9},{6,10},{7,11},{8,4},{9,5},... | collective-permute-start | bytes 393224 | tf_op jit(solution)/shard_map/ppermute | solution.py:24
  76.4 16.8 %collective-permute-start.12 = (bf16[4096,16]{0,1:T(8,128)(2,1)S(1)}, bf16[4096,16]{0,1:T(8,128)(2,1)S(1)}, u32[]{:S(2)}, u32[]{:S(2)}) collective-permute-start(bf16[4096,16]{0,1:T(8,128)(2,1)S(1)} %get-tuple-element.359), channel_id=1, source_target_pairs={{0,13},{1,12},{2,15},{3,14},{4,9},{5,8},{6,11},{7,10},{8,5},{9,4},... | collective-permute-start | bytes 393224 | tf_op jit(solution)/shard_map/ppermute | solution.py:24
  79.7 18.2 %collective-permute-start.13 = (bf16[4096,16]{0,1:T(8,128)(2,1)S(1)}, bf16[4096,16]{0,1:T(8,128)(2,1)S(1)}, u32[]{:S(2)}, u32[]{:S(2)}) collective-permute-start(bf16[4096,16]{0,1:T(8,128)(2,1)S(1)} %get-tuple-element.358), channel_id=1, source_target_pairs={{0,14},{1,15},{2,12},{3,13},{4,10},{5,11},{6,8},{7,9},{8,6},{9,7},... | collective-permute-start | bytes 393224 | tf_op jit(solution)/shard_map/ppermute | solution.py:24
  88.5 21.0 %collective-permute-start.14 = (bf16[4096,16]{0,1:T(8,128)(2,1)S(1)}, bf16[4096,16]{0,1:T(8,128)(2,1)S(1)}, u32[]{:S(2)}, u32[]{:S(2)}) collective-permute-start(bf16[4096,16]{0,1:T(8,128)(2,1)S(1)} %get-tuple-element.357), channel_id=1, source_target_pairs={{0,15},{1,14},{2,13},{3,12},{4,11},{5,10},{6,9},{7,8},{8,7},{9,6},... | collective-permute-start | bytes 393224 | tf_op jit(solution)/shard_map/ppermute | solution.py:24
  346.3 17.8 %copy-start.8 = (f32[64]{0:T(128)S(1)}, f32[64]{0:T(128)}, u32[]{:S(2)}) copy-start(f32[64]{0:T(128)} %get-tuple-element.354) | copy-start | bytes 772
  (7 other events, 10.9 us)
Sparse Core Ops, SparseCore 0:
  127.2 174.9 all-gather.2
